TPU v7x, 32 devices: a whole 2x2x4 slice. The times are simulated.
32 devices in a mesh: row: 4 (over z), col: 4 (over x, core), depth: 2 (over y).
Axes of the slice: x: 2, y: 2, z: 4, core: 2. Of those that a mesh axis runs over, the one named last changes fastest.
Arguments:
- amplitudes: float32 [14400, 4, 1200], P('row', 'depth', 'col'), may hold values from -6 to 6
- integrals: float32 [4, 1200, 4, 1200], P('depth', 'row', 'col'), may hold values from -0.375 to 0.375
- occ_energy: float32 [120], replicated, may hold values from -2 to -0.5
- vir_energy: float32 [1200], replicated, may hold values from 0.3 to 3
Outputs:
- update: float32 [14400, 4, 1200], P(('row', 'col'), 'depth')
All inputs are finite; a program needn't handle non-finite values.
Results may differ from a plain program's by a relative error of at most 0.00007.
Values sent between devices are 32-bit elements; how exact they have to be, the bound alone decides.
A program may use at most 192 MiB of HBM per device.

v0:
```python
import jax
import jax.numpy as jnp
from jax import lax
from jax.sharding import PartitionSpec as P


def body(amplitudes, integrals, occ_energy, vir_energy):
    pair_rows = amplitudes.shape[0]
    wide_amplitude = lax.all_gather(amplitudes, "col", axis=2, tiled=True)
    panel_count = integrals.shape[0]
    a_count = integrals.shape[2]
    b_count = integrals.shape[3]
    own_rows = integrals.reshape(panel_count, integrals.shape[1], a_count * b_count)
    partial_value = jnp.einsum(
        "ipd,pdn->in",
        wide_amplitude,
        lax.all_gather(own_rows, "row", axis=1, tiled=True),
        precision=lax.Precision.HIGHEST,
        preferred_element_type=jnp.float32,
    )
    partial_value = partial_value.reshape(pair_rows, a_count, b_count)
    summed = lax.psum_scatter(partial_value, "depth", scatter_dimension=2, tiled=True)
    summed = lax.all_to_all(
        lax.all_to_all(summed, "col", split_axis=0, concat_axis=1, tiled=True),
        "depth",
        split_axis=1,
        concat_axis=2,
        tiled=True,
    )
    local_pairs = summed.shape[0]
    local_a = summed.shape[1]
    occ_count = occ_energy.shape[0]
    first_pair = (
        lax.axis_index("row") * lax.axis_size("col") + lax.axis_index("col")
    ) * local_pairs
    pair_index = first_pair + jnp.arange(local_pairs, dtype=jnp.int32)
    first_index = pair_index // occ_count
    second_index = pair_index % occ_count
    occ_ids = jnp.arange(occ_count, dtype=jnp.int32)
    first_energy = jnp.sum(
        jnp.where(first_index[:, None] == occ_ids[None, :], occ_energy[None, :], 0.0), axis=1
    )
    second_energy = jnp.sum(
        jnp.where(second_index[:, None] == occ_ids[None, :], occ_energy[None, :], 0.0), axis=1
    )
    a_start = lax.axis_index("depth") * local_a
    batch_energy = lax.dynamic_slice_in_dim(vir_energy, a_start, local_a)
    pair_energy = first_energy + second_energy
    denominator = (
        pair_energy[:, None, None] - batch_energy[None, :, None] - vir_energy[None, None, :]
    )
    return summed / denominator


def solution(mesh):
    in_specs = (P("row", "depth", "col"), P("depth", "row", "col", None), P(), P())
    out_specs = P(("row", "col"), "depth", None)
    return jax.shard_map(body, mesh=mesh, in_specs=in_specs, out_specs=out_specs, check_vma=False)
```

profile of v0, /device:TPU:0, one launch (start us, length us, event | category | flops | bytes accessed | tf_op | source)
XLA Modules:
  0.0 1191.5 jit_solution(17222983624142915853)
XLA Ops:
  6.5 0.0 all-gather.6.cloned.1.call-start
  6.5 5.1 copy.22
  11.6 0.0 all-gather.6.cloned.1.call-update
  11.6 0.0 all-gather.4.cloned.1.call-start
  11.7 0.7 all-gather.4.cloned.1.call-update
  12.4 215.5 %all-gather.6.cloned.1.call-done = f32[2,1200,1,1200]{3,0,2,1:T(2,128)} async-done(((f32[2,300,1,1200]{3,0,2,1:T(2,128)}), f32[2,1200,1,1200]{3,0,2,1:T(2,128)}) %all-gather.6.cloned.1.call-update) | async-done | bytes 11520016 | tf_op jit(solution)/shard_map/all_gather | solution.py:17
  227.9 20.9 %copy.23 = f32[2,1200,1,1200]{1,3,0,2:T(8,128)} copy(f32[2,1200,1,1200]{3,0,2,1:T(2,128)} %all-gather.6.cloned.1.call-done) | data formatting | bytes 23040000 | tf_op jit(solution)/shard_map/all_gather | solution.py:17
  248.8 194.4 %all-gather.4.cloned.1.call-done = f32[3600,2,1200]{0,1,2:T(2,128)} async-done(((f32[3600,2,300]{0,1,2:T(2,128)}), f32[3600,2,1200]{0,1,2:T(2,128)}) %all-gather.4.cloned.1.call-update) | async-done | bytes 34560016 | tf_op jit(solution)/shard_map/all_gather | solution.py:9
  443.2 169.6 %fusion.3 = f32[3600,1,1200]{0,2,1:T(8,128)} fusion(f32[3600,2,1200]{0,1,2:T(2,128)} %all-gather.4.cloned.1.call-done, f32[2,1200,1,1200]{1,3,0,2:T(8,128)} %copy.23), kind=kOutput, calls=%fused_computation.2 | convolution fusion | flops 124416000000 | bytes 63360000 | tf_op jit(solution)/shard_map/ipd,pdn->in/dot_general | solution.py:14
  612.8 0.0 copy-start.2
  612.8 208.9 %fusion = f32[3600,608]{0,1:T(8,128)} fusion(f32[3600,1,1200]{0,2,1:T(8,128)} %fusion.3), kind=kCustom, calls=%all-reduce-scatter | all-reduce-scatter fusion | flops 4377601 | bytes 26035712
  821.7 0.9 slice
  822.6 2.6 collective-permute-start
  825.2 0.0 copy-done.2
  825.2 0.6 dynamic-slice.4
  826.5 1.0 collective-permute-done
  827.4 22.9 %concatenate = f32[3600,616]{0,1:T(8,128)} concatenate(f32[3600,8]{0,1:T(8,128)S(1)} %collective-permute-done, f32[3600,608]{0,1:T(8,128)} %fusion), dimensions={1} | concatenate | bytes 17740800
  850.4 7.5 dynamic-slice_bitcast_fusion
  857.9 19.8 %copy.25 = f32[3600,1,600]{2,1,0:T(1,128)} copy(f32[3600,1,600]{0,2,1:T(8,128)} %dynamic-slice_bitcast_fusion) | data formatting | bytes 17280000 | tf_op jit(solution)/shard_map/reduce_scatter | solution.py:22
  877.7 109.9 %all_to_all.36 = f32[3600,1,600]{2,1,0:T(1,128)} all-to-all(f32[3600,1,600]{2,1,0:T(1,128)} %copy.25), channel_id=1, replica_groups=mesh['row'=4,'col'=4,'depth'=2] {'col'}, dimensions={0} | all-to-all | bytes 17280000 | tf_op jit(solution)/shard_map/all_to_all | solution.py:24
  987.5 28.3 %reduce = f32[3600,600]{1,0:T(8,128)} reduce(f32[3600,1,600]{2,1,0:T(1,128)} %all_to_all.36, f32[]{:T(128)} %constant.47), dimensions={1}, to_apply=%all_to_all.26.reduce_sub_computation | reduce | bytes 17280004 | tf_op jit(solution)/shard_map/all_to_all | solution.py:24
  1015.8 9.8 all_to_all.27
  1025.7 0.0 copy-start.1
  1025.7 0.0 copy-start
  1025.7 7.4 all-to-all-start.1
  1033.1 0.0 copy-done.1
  1033.1 0.6 select_reduce_fusion
  1033.7 0.0 copy-done
  1033.7 0.1 dynamic_slice.3
  1033.8 0.1 broadcast_subtract_fusion
  1033.8 101.9 %all-to-all-done.1 = f32[900,4,600]{2,0,1:T(8,128)} async-done(((f32[900,4,600]{2,0,1:T(8,128)}), f32[900,4,600]{2,0,1:T(8,128)}, u32[]{:S(2)}, u32[]{:S(2)}) %all-to-all-start.1) | async-done | bytes 8640032 | tf_op jit(solution)/shard_map/all_to_all | solution.py:23
  1135.8 19.9 %copy.26 = f32[900,2,2,600]{3,2,0,1:T(2,128)} copy(f32[900,2,2,600]{3,0,1,2:T(8,128)} %bitcast.6) | data formatting | bytes 17280000 | tf_op jit(solution)/shard_map/all_to_all | solution.py:23
  1155.6 15.3 %all_to_all.33 = f32[900,2,1200]{2,0,1:T(8,128)} reshape(f32[900,2,2,600]{3,2,0,1:T(2,128)} %copy.26) | data formatting | bytes 17280000 | tf_op jit(solution)/shard_map/all_to_all | solution.py:23
  1170.9 4.9 subtract_divide_fusion
  1175.8 8.8 copy.27
  (2 shorter events, 0.0 us)
Async XLA Ops:
  6.5 221.4 %all-gather.6.cloned.1.call-start = ((), (), s32[]{:S(2)}) async-start(), calls=%async_computation.3 | async-start | bytes 15360000 | tf_op jit(solution)/shard_map/all_gather | solution.py:17
  11.6 431.5 %all-gather.4.cloned.1.call-start = ((), (), s32[]{:S(2)}) async-start(), calls=%async_computation.2 | async-start | bytes 44544000 | tf_op jit(solution)/shard_map/all_gather | solution.py:9
  612.8 212.5 %copy-start.2 = (u32[32]{0:T(128)S(1)}, u32[32]{0:T(128)}, u32[]{:S(2)}) copy-start(u32[32]{0:T(128)} %constant.45) | copy-start | bytes 388
  822.6 4.8 collective-permute-start
  1025.7 7.4 copy-start.1
  1025.7 8.0 copy-start
  1025.7 110.1 %all-to-all-start.1 = ((f32[900,4,600]{2,0,1:T(8,128)}), f32[900,4,600]{2,0,1:T(8,128)}, u32[]{:S(2)}, u32[]{:S(2)}) async-start(f32[900,4,600]{2,0,1:T(8,128)} %bitcast.24), calls=%async_computation.1 | async-start | bytes 18513920 | tf_op jit(solution)/shard_map/all_to_all | solution.py:23
Sparse Core Ops, SparseCore 0:
  11.8 216.0 all-gather.5
  229.5 213.6 all-gather.3
where the time goes:
time: 1190 us
  waiting for transfers between devices  513 us (43%)
  blocking collectives  319 us (27%)
  matrix products  170 us (14%)
  local copies, waits for them, and re-layouts  132 us (11%)
  other arithmetic  33.9 us (3%)
  between operations  14.1 us (1%)
    all_gather x1, waiting for transfers between devices, body(): lax.all_gather(own_rows, 'row', axis=1, tiled=True)  215 us
    unnamed x1, blocking collectives  209 us
    all_gather x1, waiting for transfers between devices, body(): wide_amplitude = lax.all_gather(amplitudes, 'col', axis=2, tiled=True)  194 us
    dot_general x1, matrix products, body(): jnp.einsum('ipd,pdn->in', wide_amplitude, lax.all_gather(own_rows, 'row',...  170 us
    all_to_all x1, blocking collectives, body(): lax.all_to_all(summed, 'col', split_axis=0, concat_axis=1, tiled=True)  110 us
    all_to_all x1, waiting for transfers between devices, body(): lax.all_to_all(lax.all_to_all(summed, 'col', split_axis=0, concat_axis=1,...  102 us
    unnamed x11, local copies, waits for them, and re-layouts  37.1 us
    all_to_all x2, local copies, waits for them, and re-layouts, body(): lax.all_to_all(lax.all_to_all(summed, 'col', split_axis=0, concat_axis=1,...  35.2 us
  transfers between devices with their start and end apart: 4, of which 4 were waited for; matrix products, arithmetic and copies ran while one was open for 2% of the time, Pallas kernels for 0%

commit v1 on v0

--- a/solution.py
+++ b/solution.py
@@ -2,6 +2,22 @@
 import jax.numpy as jnp
 from jax import lax
 from jax.sharding import PartitionSpec as P
+
+
+def ring_product(x, axis, dim, term):
+    size, position, extent = (lax.axis_size(axis), lax.axis_index(axis), x.shape[dim])
+    ahead = [(i, (i + 1) % size) for i in range(size)]
+    left = [(i, (i - 1) % size) for i in range(size)]
+    halfway = size // 2
+    from_left = from_right = x
+    total = term(x, position * extent)
+    for lap in range(1, halfway + 1):
+        from_left = lax.ppermute(from_left, axis, ahead)
+        if lap < size - halfway:
+            from_right = lax.ppermute(from_right, axis, left)
+            total = total + term(from_right, (position + lap) % size * extent)
+        total = total + term(from_left, (position - lap) % size * extent)
+    return total
 
 
 def body(amplitudes, integrals, occ_energy, vir_energy):
@@ -11,12 +27,17 @@
     a_count = integrals.shape[2]
     b_count = integrals.shape[3]
     own_rows = integrals.reshape(panel_count, integrals.shape[1], a_count * b_count)
-    partial_value = jnp.einsum(
-        "ipd,pdn->in",
-        wide_amplitude,
-        lax.all_gather(own_rows, "row", axis=1, tiled=True),
-        precision=lax.Precision.HIGHEST,
-        preferred_element_type=jnp.float32,
+    partial_value = ring_product(
+        own_rows,
+        "row",
+        1,
+        lambda part, at: jnp.einsum(
+            "ipd,pdn->in",
+            lax.dynamic_slice_in_dim(wide_amplitude, at, part.shape[1], axis=2),
+            part,
+            precision=lax.Precision.HIGHEST,
+            preferred_element_type=jnp.float32,
+        ),
     )
     partial_value = partial_value.reshape(pair_rows, a_count, b_count)
     summed = lax.psum_scatter(partial_value, "depth", scatter_dimension=2, tiled=True)

time: 1190 us -> 1050 us (0.88)
  waiting for transfers between devices: 513 us -> 313 us
  matrix products: 170 us -> 207 us
    all_gather x1 -> x0, waiting for transfers between devices: 215 us -> none  [body(): lax.all_gather(own_rows, 'row', axis=1, tiled=True)]
    ppermute x0 -> x3, waiting for transfers between devices: none -> 67.7 us  [the longest x2 67.7 us: ring_product(): from_left = lax.ppermute(from_left, axis, ahead)]
    all_gather x1, waiting for transfers between devices: 194 us -> 142 us  [body(): wide_amplitude = lax.all_gather(amplitudes, 'col', axis=2, tiled=True)]
    dot_general x1 -> x4, matrix products: 170 us -> 207 us  [body(): jnp.einsum('ipd,pdn->in', lax.dynamic_slice_in_dim(wide_amplitude, at, pa...]
    dynamic_slice x0 -> x1, local copies, waits for them, and re-layouts: none -> 30.6 us  [body(): lax.dynamic_slice_in_dim(wide_amplitude, at, part.shape[1], axis=2)]
    all_gather x1 -> x0, local copies, waits for them, and re-layouts: 20.9 us -> none  [body(): lax.all_gather(own_rows, 'row', axis=1, tiled=True)]
    unnamed x11 -> x25, local copies, waits for them, and re-layouts: 37.1 us -> 33.4 us
  transfers between devices with their start and end apart: 4 -> 6, of which waited for: 4 -> 4; matrix products, arithmetic and copies ran while one was open for 2% -> 18% of each run, Pallas kernels for 0% -> 0%
where the time goes in v1:
time: 1050 us; the launch traced here: 1040 us
  blocking collectives  319 us (30%)
  waiting for transfers between devices  313 us (30%)
  matrix products  207 us (20%)
  local copies, waits for them, and re-layouts  142 us (14%)
  other arithmetic  33.9 us (3%)
  starting transfers between devices  14.9 us (1%)
  between operations  14.4 us (1%)
    unnamed x1, blocking collectives  209 us
    dot_general x4, matrix products, body(): jnp.einsum('ipd,pdn->in', lax.dynamic_slice_in_dim(wide_amplitude, at, pa...  207 us
    all_gather x1, waiting for transfers between devices, body(): wide_amplitude = lax.all_gather(amplitudes, 'col', axis=2, tiled=True)  142 us
    all_to_all x1, blocking collectives, body(): lax.all_to_all(summed, 'col', split_axis=0, concat_axis=1, tiled=True)  110 us
    all_to_all x1, waiting for transfers between devices, body(): lax.all_to_all(lax.all_to_all(summed, 'col', split_axis=0, concat_axis=1,...  102 us
    ppermute x2, waiting for transfers between devices, ring_product(): from_left = lax.ppermute(from_left, axis, ahead)  67.7 us
    all_to_all x2, local copies, waits for them, and re-layouts, body(): lax.all_to_all(lax.all_to_all(summed, 'col', split_axis=0, concat_axis=1,...  35.2 us
    unnamed x25, local copies, waits for them, and re-layouts  33.4 us
  transfers between devices with their start and end apart: 6, of which 4 were waited for; matrix products, arithmetic and copies ran while one was open for 18% of the time, Pallas kernels for 0%

profile of v1, /device:TPU:0, one launch (start us, length us, event | category | flops | bytes accessed | tf_op | source)
XLA Modules:
  0.0 1043.6 jit_solution(12742498446848905641)
XLA Ops:
  6.5 0.0 copy-start
  6.5 0.0 all-gather.2.cloned.1.call-start
  6.5 0.7 all-gather.2.cloned.1.call-update
  7.3 1.1 copy-done
  8.4 0.2 copy.61
  8.6 4.0 copy.27
  12.6 3.1 collective-permute-start.1
  15.7 2.0 collective-permute-start
  17.7 67.7 %collective-permute-done.1 = f32[2,300,1200]{2,0,1:T(2,128)} collective-permute-done((f32[2,300,1200]{2,0,1:T(2,128)}, f32[2,300,1200]{2,0,1:T(2,128)}, u32[]{:S(2)}, u32[]{:S(2)}) %collective-permute-start.1) | collective-permute-done | bytes 2880032 | tf_op jit(solution)/shard_map/ppermute | solution.py:15
  85.4 0.0 collective-permute-start.2
  85.4 141.7 %all-gather.2.cloned.1.call-done = f32[3600,2,1200]{0,1,2:T(2,128)} async-done(((f32[3600,2,300]{0,1,2:T(2,128)}), f32[3600,2,1200]{0,1,2:T(2,128)}) %all-gather.2.cloned.1.call-update) | async-done | bytes 34560016 | tf_op jit(solution)/shard_map/all_gather | solution.py:25
  227.2 30.6 %constant_dynamic-slice_fusion = (f32[3600,2,300]{0,1,2:T(2,128)}, f32[3600,2,300]{0,1,2:T(2,128)}, f32[3600,2,300]{0,1,2:T(2,128)}, f32[3600,2,300]{0,1,2:T(2,128)}) fusion(f32[3600,2,1200]{0,1,2:T(2,128)} %all-gather.2.cloned.1.call-done, s32[]{:T(128)S(6)} %select_n.62, s32[]{:T(128)S(6)} %select_n.60, s32[]{:T(128)S(6)} %select_n.58, s32[]{:T(128)S(6)} %select_n.56), kind=kLoop, calls=%fused_computation.31 | loop fusion | bytes 69120016 | tf_op jit(solution)/shard_map/dynamic_slice | solution.py:36
  257.8 0.0 slice-start.3
  257.8 0.0 slice-start.4
  257.8 50.4 %fusion.7 = f32[3600,1200,1]{0,1,2:T(8,128)} fusion(f32[3600,2,300]{0,1,2:T(2,128)} %get-tuple-element.10, f32[2,300,1,1200]{3,2,1,0:T(1,128)} %param.5), kind=kOutput, calls=%fused_computation.10 | convolution fusion | flops 31104000000 | bytes 28800000 | tf_op jit(solution)/shard_map/ipd,pdn->in/dot_general | solution.py:34
  308.2 0.0 slice-start.5
  308.2 0.0 slice-start
  308.2 0.0 slice-start.1
  308.2 51.2 %fusion.3 = f32[3600,1200,1]{0,1,2:T(8,128)} fusion(f32[3600,2,300]{0,1,2:T(2,128)} %get-tuple-element.8, f32[2,300,1200]{2,0,1:T(2,128)} %collective-permute-done.1), kind=kOutput, calls=%fused_computation.6 | convolution fusion | flops 31104000000 | bytes 28800000 | tf_op jit(solution)/shard_map/ipd,pdn->in/dot_general | solution.py:34
  359.4 0.0 collective-permute-done
  359.4 0.0 slice-done.3
  359.4 0.0 slice-done.4
  359.5 0.0 slice-done.5
  359.5 0.0 slice-start.2
  359.5 49.6 %fusion.5 = f32[3600,1200,1]{0,1,2:T(8,128)} fusion(f32[3600,2,300]{0,1,2:T(2,128)S(1)} %bitcast.43, f32[2,300,1200]{2,0,1:T(2,128)} %collective-permute-done), kind=kOutput, calls=%fused_computation.8 | convolution fusion | flops 31104000000 | bytes 28800000 | tf_op jit(solution)/shard_map/ipd,pdn->in/dot_general | solution.py:34
  409.1 0.0 collective-permute-done.2
  409.1 0.0 slice-done
  409.1 0.0 slice-done.1
  409.1 0.0 slice-done.2
  409.1 55.4 %fusion.1 = f32[3600,1,1200]{0,2,1:T(8,128)} fusion(f32[3600,1200,1]{0,1,2:T(8,128)} %fusion.3, f32[3600,1200,1]{0,1,2:T(8,128)} %fusion.5, f32[3600,1200,1]{0,1,2:T(8,128)} %fusion.7, f32[3600,2,300]{0,1,2:T(2,128)S(1)} %bitcast.39, f32[2,300,1200]{2,0,1:T(2,128)S(1)} %collective-permute-done.2), kind=kOutput, calls=%fused_computation.1 | convolution fusion | flops 31116959744 | bytes 80640000 | tf_op jit(solution)/shard_map/ipd,pdn->in/dot_general | solution.py:34
  464.5 0.0 copy-start.3
  464.5 209.0 %fusion = f32[3600,608]{0,1:T(8,128)} fusion(f32[3600,1,1200]{0,2,1:T(8,128)} %fusion.1), kind=kCustom, calls=%all-reduce-scatter | all-reduce-scatter fusion | flops 4377601 | bytes 26035712
  673.5 0.9 slice
  674.4 2.4 collective-permute-start.3
  676.8 0.0 copy-done.3
  676.8 0.6 dynamic-slice.4
  678.1 1.1 collective-permute-done.3
  679.2 22.9 %concatenate = f32[3600,616]{0,1:T(8,128)} concatenate(f32[3600,8]{0,1:T(8,128)S(1)} %collective-permute-done.3, f32[3600,608]{0,1:T(8,128)} %fusion), dimensions={1} | concatenate | bytes 17740800
  702.1 7.6 dynamic-slice_bitcast_fusion
  709.7 19.8 %copy.34 = f32[3600,1,600]{2,1,0:T(1,128)} copy(f32[3600,1,600]{0,2,1:T(8,128)} %dynamic-slice_bitcast_fusion) | data formatting | bytes 17280000 | tf_op jit(solution)/shard_map/reduce_scatter | solution.py:43
  729.5 110.0 %all_to_all.36 = f32[3600,1,600]{2,1,0:T(1,128)} all-to-all(f32[3600,1,600]{2,1,0:T(1,128)} %copy.34), channel_id=1, replica_groups=mesh['row'=4,'col'=4,'depth'=2] {'col'}, dimensions={0} | all-to-all | bytes 17280000 | tf_op jit(solution)/shard_map/all_to_all | solution.py:45
  839.5 28.3 %reduce = f32[3600,600]{1,0:T(8,128)} reduce(f32[3600,1,600]{2,1,0:T(1,128)} %all_to_all.36, f32[]{:T(128)} %constant.71), dimensions={1}, to_apply=%all_to_all.26.reduce_sub_computation | reduce | bytes 17280004 | tf_op jit(solution)/shard_map/all_to_all | solution.py:45
  867.8 9.8 all_to_all.27
  877.6 0.0 copy-start.2
  877.6 0.0 copy-start.1
  877.6 7.4 all-to-all-start.1
  885.0 0.0 copy-done.2
  885.1 0.6 select_reduce_fusion
  885.7 0.0 copy-done.1
  885.7 0.1 dynamic_slice.19
  885.8 0.1 broadcast_subtract_fusion
  885.8 101.9 %all-to-all-done.1 = f32[900,4,600]{2,0,1:T(8,128)} async-done(((f32[900,4,600]{2,0,1:T(8,128)}), f32[900,4,600]{2,0,1:T(8,128)}, u32[]{:S(2)}, u32[]{:S(2)}) %all-to-all-start.1) | async-done | bytes 8640032 | tf_op jit(solution)/shard_map/all_to_all | solution.py:44
  987.7 19.9 %copy.35 = f32[900,2,2,600]{3,2,0,1:T(2,128)} copy(f32[900,2,2,600]{3,0,1,2:T(8,128)} %bitcast.8) | data formatting | bytes 17280000 | tf_op jit(solution)/shard_map/all_to_all | solution.py:44
  1007.6 15.3 %all_to_all.33 = f32[900,2,1200]{2,0,1:T(8,128)} reshape(f32[900,2,2,600]{3,2,0,1:T(2,128)} %copy.35) | data formatting | bytes 17280000 | tf_op jit(solution)/shard_map/all_to_all | solution.py:44
  1022.9 4.9 subtract_divide_fusion
  1027.8 8.8 copy.36
  (4 shorter events, 0.0 us)
Async XLA Ops:
  6.5 1.9 copy-start
  6.5 220.6 %all-gather.2.cloned.1.call-start = ((), (), s32[]{:S(2)}) async-start(), calls=%async_computation.2 | async-start | bytes 44544000 | tf_op jit(solution)/shard_map/all_gather | solution.py:25
  12.6 72.8 %collective-permute-start.1 = (f32[2,300,1200]{2,0,1:T(2,128)}, f32[2,300,1200]{2,0,1:T(2,128)}, u32[]{:S(2)}, u32[]{:S(2)}) collective-permute-start(f32[2,300,1200]{2,0,1:T(2,128)} %copy.27), channel_id=1, source_target_pairs={{0,8},{8,16},{16,24},{24,0},{1,9},{9,17},{17,25},{25,1},{2,10},{10... | collective-permute-start | bytes 8640008 | tf_op jit(solution)/shard_map/ppermute | solution.py:15
  15.7 343.7 %collective-permute-start = (f32[2,300,1200]{2,0,1:T(2,128)}, f32[2,300,1200]{2,0,1:T(2,128)}, u32[]{:S(2)}, u32[]{:S(2)}) collective-permute-start(f32[2,300,1200]{2,0,1:T(2,128)} %copy.27), channel_id=1, source_target_pairs={{0,24},{8,0},{16,8},{24,16},{1,25},{9,1},{17,9},{25,17},{2,26},{10... | collective-permute-start | bytes 8640008 | tf_op jit(solution)/shard_map/ppermute | solution.py:17
  85.4 323.6 %collective-permute-start.2 = (f32[2,300,1200]{2,0,1:T(2,128)}, f32[2,300,1200]{2,0,1:T(2,128)S(1)}, u32[]{:S(2)}, u32[]{:S(2)}) collective-permute-start(f32[2,300,1200]{2,0,1:T(2,128)} %collective-permute-done.1), channel_id=1, source_target_pairs={{0,8},{8,16},{16,24},{24,0},{1,9},{9,17},{17,25},{25,1},{2,10},{10... | collective-permute-start | bytes 8640008 | tf_op jit(solution)/shard_map/ppermute | solution.py:15
  257.8 101.7 %slice-start.3 = ((s8[8908800]{0:T(1024)(128)(4,1)}), s8[4194304]{0:T(1024)(128)(4,1)S(1)}, s32[]{:S(2)}) async-start(s8[8908800]{0:T(1024)(128)(4,1)} %bitcast.42), calls=%async_computation.6 | async-start | bytes 8388608
  257.8 101.7 %slice-start.4 = ((s8[8908800]{0:T(1024)(128)(4,1)}), s8[4194304]{0:T(1024)(128)(4,1)S(1)}, s32[]{:S(2)}) async-start(s8[8908800]{0:T(1024)(128)(4,1)} %bitcast.42), calls=%async_computation.7 | async-start | bytes 8388608
  308.2 51.2 %slice-start.5 = ((s8[8908800]{0:T(1024)(128)(4,1)}), s8[520192]{0:T(1024)(128)(4,1)S(1)}, s32[]{:S(2)}) async-start(s8[8908800]{0:T(1024)(128)(4,1)} %bitcast.42), calls=%async_computation.8 | async-start | bytes 1040384
  308.2 100.9 %slice-start = ((s8[8908800]{0:T(1024)(128)(4,1)}), s8[4194304]{0:T(1024)(128)(4,1)S(1)}, s32[]{:S(2)}) async-start(s8[8908800]{0:T(1024)(128)(4,1)} %bitcast.38), calls=%async_computation.3 | async-start | bytes 8388608
  308.2 100.9 %slice-start.1 = ((s8[8908800]{0:T(1024)(128)(4,1)}), s8[4194304]{0:T(1024)(128)(4,1)S(1)}, s32[]{:S(2)}) async-start(s8[8908800]{0:T(1024)(128)(4,1)} %bitcast.38), calls=%async_computation.4 | async-start | bytes 8388608
  359.5 49.6 %slice-start.2 = ((s8[8908800]{0:T(1024)(128)(4,1)}), s8[520192]{0:T(1024)(128)(4,1)S(1)}, s32[]{:S(2)}) async-start(s8[8908800]{0:T(1024)(128)(4,1)} %bitcast.38), calls=%async_computation.5 | async-start | bytes 1040384
  464.5 212.3 %copy-start.3 = (u32[32]{0:T(128)S(1)}, u32[32]{0:T(128)}, u32[]{:S(2)}) copy-start(u32[32]{0:T(128)} %constant.69) | copy-start | bytes 388
  674.4 4.8 collective-permute-start.3
  877.6 7.4 copy-start.2
  877.6 8.1 copy-start.1
  877.6 110.1 %all-to-all-start.1 = ((f32[900,4,600]{2,0,1:T(8,128)}), f32[900,4,600]{2,0,1:T(8,128)}, u32[]{:S(2)}, u32[]{:S(2)}) async-start(f32[900,4,600]{2,0,1:T(8,128)} %bitcast.40), calls=%async_computation.1 | async-start | bytes 18513920 | tf_op jit(solution)/shard_map/all_to_all | solution.py:44
Sparse Core Ops, SparseCore 0:
  8.9 218.2 all-gather.1
